TPU v7x, 256 devices: a whole 4x4x8 slice. The times are simulated.
256 devices in a mesh: section: 16 (over z, core), ctx: 16 (over x, y).
Axes of the slice: x: 4, y: 4, z: 8, core: 2. Of those that a mesh axis runs over, the one named last changes fastest.
Arguments:
- queries: bfloat16 [16, 2560, 32, 128], P('section', 'ctx'), may hold values from -30 to 30
- key_rows: bfloat16 [16, 2560, 16, 128], P('section', 'ctx'), may hold values from -6 to 6
- stored_value_rows: bfloat16 [16, 2560, 16, 128], P('section', 'ctx'), may hold values from -6 to 6
- grad_out: bfloat16 [16, 2560, 32, 128], P('section', 'ctx'), may hold values from -6 to 6
Outputs:
- query_gradient_rows: bfloat16 [16, 2560, 32, 128], P('section', 'ctx')
- grad_keys: bfloat16 [16, 2560, 16, 128], P('section', 'ctx')
- grad_values: bfloat16 [16, 2560, 16, 128], P('section', 'ctx')
All inputs are finite; a program needn't handle non-finite values.
Results may differ from a plain program's by a relative error of at most 0.009.
Values may be sent and summed in bfloat16 or wider, within the bound.
A program may use at most 128 MiB of HBM per device.

v0:
```python
import jax
import jax.numpy as jnp
from jax import lax
from jax.sharding import PartitionSpec as P

WINDOW = 1024
QBLOCK = 256


query_scale = 168.0 ** (-0.5)
masked_value = -1e30


def from_behind(value, axis, steps):
    count = lax.axis_size(axis)
    pairs = [(source, (source + steps) % count) for source in range(count)]
    return lax.ppermute(value, axis, pairs)


def band_terms(query_block, key_block, value_block, grad_block, query_places, key_places):
    scores = (
        jnp.einsum("bngd,knd->ngbk", query_block, key_block, preferred_element_type=jnp.float32)
        * query_scale
    )
    allowed = (
        (key_places[None, :] <= query_places[:, None])
        & (key_places[None, :] > query_places[:, None] - WINDOW)
        & (key_places[None, :] >= 0)
    )
    scores = jnp.where(allowed, scores, masked_value)
    row_max = jnp.max(scores, axis=-1, keepdims=True)
    weights = jnp.exp(scores - row_max)
    probs_full = weights / jnp.sum(weights, axis=-1, keepdims=True)
    probs_half = probs_full.astype(jnp.bfloat16)
    grad_probs = jnp.einsum(
        "bngd,knd->ngbk", grad_block, value_block, preferred_element_type=jnp.float32
    )
    row_dot = jnp.sum(probs_full * grad_probs, axis=-1, keepdims=True)
    grad_scores = (probs_full * (grad_probs - row_dot)).astype(jnp.bfloat16)
    grad_query = (
        jnp.einsum("ngbk,knd->bngd", grad_scores, key_block, preferred_element_type=jnp.float32)
        * query_scale
    )
    grad_key = (
        jnp.einsum("ngbk,bngd->knd", grad_scores, query_block, preferred_element_type=jnp.float32)
        * query_scale
    )
    grad_value = jnp.einsum(
        "ngbk,bngd->knd", probs_half, grad_block, preferred_element_type=jnp.float32
    )
    return (grad_query, grad_key, grad_value)


def heads_grads(queries_heads, keys_heads, values_heads, grads_heads):
    length = queries_heads.shape[1]
    groups = queries_heads.shape[3]
    head_size = keys_heads.shape[4]
    per_group = queries_heads.shape[4] // head_size
    query_all = queries_heads[0, :, 0].reshape(length, groups, per_group, head_size)
    grad_all = grads_heads[0, :, 0].reshape(length, groups, per_group, head_size)
    padding = jnp.zeros((WINDOW, groups, head_size), jnp.bfloat16)
    key_all = jnp.concatenate([padding, keys_heads[0, :, 0]], axis=0)
    value_all = jnp.concatenate([padding, values_heads[0, :, 0]], axis=0)
    span = QBLOCK + WINDOW

    def one_block(block_num, carry):
        grad_query_all, key_gradient_total, grad_value_acc = carry
        first_row = block_num * QBLOCK
        query_places = first_row + jnp.arange(QBLOCK, dtype=jnp.int32)
        key_places = first_row - WINDOW + jnp.arange(span, dtype=jnp.int32)
        terms = band_terms(
            lax.dynamic_slice_in_dim(query_all, first_row, QBLOCK, 0),
            lax.dynamic_slice_in_dim(key_all, first_row, span, 0),
            lax.dynamic_slice_in_dim(value_all, first_row, span, 0),
            lax.dynamic_slice_in_dim(grad_all, first_row, QBLOCK, 0),
            query_places,
            key_places,
        )
        grad_query_all = lax.dynamic_update_slice_in_dim(
            grad_query_all, terms[0].astype(jnp.bfloat16), first_row, 0
        )
        old_keys = lax.dynamic_slice_in_dim(key_gradient_total, first_row, span, 0)
        key_gradient_total = lax.dynamic_update_slice_in_dim(
            key_gradient_total, old_keys + terms[1], first_row, 0
        )
        old_values = lax.dynamic_slice_in_dim(grad_value_acc, first_row, span, 0)
        grad_value_acc = lax.dynamic_update_slice_in_dim(
            grad_value_acc, old_values + terms[2], first_row, 0
        )
        return (grad_query_all, key_gradient_total, grad_value_acc)

    start_state = (
        jnp.zeros((length, groups, per_group, head_size), jnp.bfloat16),
        jnp.zeros((length + WINDOW, groups, head_size), jnp.float32),
        jnp.zeros((length + WINDOW, groups, head_size), jnp.float32),
    )
    finals = lax.fori_loop(0, length // QBLOCK, one_block, start_state)
    grad_query_out = finals[0].reshape(1, length, 1, groups, per_group * head_size)
    grad_key_out = finals[1][WINDOW:].astype(jnp.bfloat16).reshape(1, length, 1, groups, head_size)
    grad_value_out = (
        finals[2][WINDOW:].astype(jnp.bfloat16).reshape(1, length, 1, groups, head_size)
    )
    return (grad_query_out, grad_key_out, grad_value_out)


def body(queries, key_rows, stored_value_rows, grad_out):
    incoming = from_behind(grad_out, "section", -1)
    local_rows = queries.shape[1]
    heads = queries.shape[2]
    head_size = queries.shape[3]
    kv_heads = key_rows.shape[2]
    per_group = heads // kv_heads
    members = lax.axis_size("ctx")
    groups_dev = kv_heads // members
    packed_queries = queries.reshape(1, local_rows, members, groups_dev, per_group * head_size)
    packed_grads = incoming.reshape(1, local_rows, members, groups_dev, per_group * head_size)
    packed_keys = key_rows.reshape(1, local_rows, members, groups_dev, head_size)
    packed_values = stored_value_rows.reshape(1, local_rows, members, groups_dev, head_size)
    results = (lambda pieces: heads_grads(*pieces))(
        (
            lax.all_to_all(packed_queries, "ctx", split_axis=2, concat_axis=1, tiled=True),
            lax.all_to_all(packed_keys, "ctx", split_axis=2, concat_axis=1, tiled=True),
            lax.all_to_all(packed_values, "ctx", split_axis=2, concat_axis=1, tiled=True),
            lax.all_to_all(packed_grads, "ctx", split_axis=2, concat_axis=1, tiled=True),
        )
    )
    returned = (
        lax.all_to_all(results[0], "ctx", split_axis=1, concat_axis=2, tiled=True),
        lax.all_to_all(results[1], "ctx", split_axis=1, concat_axis=2, tiled=True),
        lax.all_to_all(results[2], "ctx", split_axis=1, concat_axis=2, tiled=True),
    )
    query_gradient_rows = returned[0].reshape(1, local_rows, heads, head_size)
    grad_keys = returned[1].reshape(1, local_rows, kv_heads, head_size)
    grad_values = returned[2].reshape(1, local_rows, kv_heads, head_size)
    return (query_gradient_rows, grad_keys, grad_values)


def solution(mesh):
    return jax.shard_map(
        body,
        mesh=mesh,
        in_specs=(
            P("section", "ctx", None, None),
            P("section", "ctx", None, None),
            P("section", "ctx", None, None),
            P("section", "ctx", None, None),
        ),
        out_specs=(
            P("section", "ctx", None, None),
            P("section", "ctx", None, None),
            P("section", "ctx", None, None),
        ),
        check_vma=False,
    )
```

profile of v0, /device:TPU:96, one launch (start us, length us, event | category | flops | bytes accessed | tf_op | source)
XLA Modules:
  0.0 375.4 jit_solution(11022894296704558702)
XLA Ops:
  2.8 7.0 %all-to-all-start = ((bf16[1,160,16,1,128]{4,1,3,0,2:T(8,128)(2,1)}), bf16[1,160,16,1,128]{4,1,3,0,2:T(8,128)(2,1)S(1)}, u32[]{:S(2)}, u32[]{:S(2)}) async-start(bf16[1,160,16,1,128]{4,1,3,0,2:T(8,128)(2,1)} %bitcast.135), calls=%async_computation | async-start | bytes 1310720 | tf_op jit(solution)/shard_map/all_to_all | solution.py:122
  10.9 11.9 %all-to-all-done = bf16[1,160,16,1,128]{4,1,3,0,2:T(8,128)(2,1)S(1)} async-done(((bf16[1,160,16,1,128]{4,1,3,0,2:T(8,128)(2,1)}), bf16[1,160,16,1,128]{4,1,3,0,2:T(8,128)(2,1)S(1)}, u32[]{:S(2)}, u32[]{:S(2)}) %all-to-all-start) | async-done | bytes 655392 | tf_op jit(solution)/shard_map/all_to_all | solution.py:122
  22.7 3.6 all-to-all-start.2
  30.2 7.8 %all-to-all-done.2 = bf16[1,160,16,1,128]{4,1,3,0,2:T(8,128)(2,1)S(1)} async-done(((bf16[1,160,16,1,128]{4,1,3,0,2:T(8,128)(2,1)}), bf16[1,160,16,1,128]{4,1,3,0,2:T(8,128)(2,1)S(1)}, u32[]{:S(2)}, u32[]{:S(2)}) %all-to-all-start.2) | async-done | bytes 655392 | tf_op jit(solution)/shard_map/all_to_all | solution.py:123
  38.0 3.7 all-to-all-start.1
  45.6 13.8 %all-to-all-done.1 = bf16[1,160,16,1,256]{4,1,3,0,2:T(8,128)(2,1)S(1)} async-done(((bf16[1,160,16,1,256]{4,1,3,0,2:T(8,128)(2,1)}), bf16[1,160,16,1,256]{4,1,3,0,2:T(8,128)(2,1)S(1)}, u32[]{:S(2)}, u32[]{:S(2)}) %all-to-all-start.1) | async-done | bytes 1310752 | tf_op jit(solution)/shard_map/all_to_all | solution.py:121
  59.4 3.9 %all-to-all-start.3 = ((bf16[1,160,16,1,256]{4,1,3,0,2:T(8,128)(2,1)}), bf16[1,160,16,1,256]{4,1,3,0,2:T(8,128)(2,1)S(1)}, u32[]{:S(2)}, u32[]{:S(2)}) async-start(bf16[1,160,16,1,256]{4,1,3,0,2:T(8,128)(2,1)} %copy.75), calls=%async_computation.3 | async-start | bytes 2621440 | tf_op jit(solution)/shard_map/all_to_all | solution.py:124
  66.9 15.5 %all-to-all-done.3 = bf16[1,160,16,1,256]{4,1,3,0,2:T(8,128)(2,1)S(1)} async-done(((bf16[1,160,16,1,256]{4,1,3,0,2:T(8,128)(2,1)}), bf16[1,160,16,1,256]{4,1,3,0,2:T(8,128)(2,1)S(1)}, u32[]{:S(2)}, u32[]{:S(2)}) %all-to-all-start.3) | async-done | bytes 1310752 | tf_op jit(solution)/shard_map/all_to_all | solution.py:124
  87.6 166.9 %while.20 = (s32[]{:T(128)}, bf16[2560,1,2,128]{0,3,2,1:T(8,128)(2,1)}, f32[3584,1,128]{2,0,1:T(8,128)}, f32[3584,1,128]{2,0,1:T(8,128)}, bf16[3584,1,128]{2,0,1...) while((s32[]{:T(128)}, ...), condition=%wide.region_4.5_spmd, body=%wide.region_0.4_spmd.sunk | while | flops 851938304 | bytes 48732976 | solution.py:97
  98.3 2.4 fusion.47
  115.0 2.4 fusion.47
  131.7 2.4 fusion.47
  148.3 2.4 fusion.47
  165.0 2.4 fusion.47
  181.8 2.4 fusion.47
  198.5 2.4 fusion.47
  215.2 2.4 fusion.47
  231.8 2.4 fusion.47
  248.5 2.4 fusion.47
  256.4 10.5 %copy.121 = bf16[1,2560,1,1,128]{4,3,2,0,1:T(2,128)(2,1)S(1)} copy(bf16[1,2560,1,1,128]{4,1,3,2,0:T(8,128)(2,1)S(1)} %get-tuple-element.294) | data formatting | bytes 1310720 | tf_op jit(solution)/shard_map/reshape | solution.py:99
  267.5 14.3 %reduce.22 = bf16[2560,128]{1,0:T(8,128)(2,1)S(1)} reduce(bf16[2560,1,1,1,128]{4,3,2,1,0:T(2,128)(2,1)S(1)} %bitcast.172, bf16[]{:T(256)} %broadcast.133), dimensions={1,2,3}, to_apply=%bitcast.137.reduce_sub_computation | reduce | bytes 1310722
  282.8 3.8 %all-to-all-start.5 = ((bf16[16,2,10240]{2,1,0:T(2,128)(2,1)}), bf16[16,2,10240]{2,1,0:T(2,128)(2,1)S(1)}, u32[]{:S(2)}, u32[]{:S(2)}) async-start(bf16[16,2,10240]{2,1,0:T(2,128)(2,1)} %reshape.203), calls=%async_computation.5 | async-start | bytes 1310720 | tf_op jit(solution)/shard_map/all_to_all | solution.py:129
  286.6 10.5 %copy.120 = bf16[1,2560,1,1,128]{4,3,2,0,1:T(2,128)(2,1)S(1)} copy(bf16[1,2560,1,1,128]{4,1,3,2,0:T(8,128)(2,1)S(1)} %get-tuple-element.295) | data formatting | bytes 1310720 | tf_op jit(solution)/shard_map/reshape | solution.py:101
  297.1 14.3 %reduce.23 = bf16[2560,128]{1,0:T(8,128)(2,1)S(1)} reduce(bf16[2560,1,1,1,128]{4,3,2,1,0:T(2,128)(2,1)S(1)} %bitcast.173, bf16[]{:T(256)} %broadcast.133), dimensions={1,2,3}, to_apply=%bitcast.136.reduce_sub_computation | reduce | bytes 1310722
  312.4 7.0 %all-to-all-start.6 = ((bf16[16,2,10240]{2,1,0:T(2,128)(2,1)}), bf16[16,2,10240]{2,1,0:T(2,128)(2,1)}, u32[]{:S(2)}, u32[]{:S(2)}) async-start(bf16[16,2,10240]{2,1,0:T(2,128)(2,1)} %reshape.205), calls=%async_computation.6 | async-start | bytes 1310720 | tf_op jit(solution)/shard_map/all_to_all | solution.py:130
  319.4 5.8 %copy.78 = bf16[1,2560,1,1,256]{4,3,2,0,1:T(2,128)(2,1)S(1)} copy(bf16[1,2560,1,1,256]{1,4,3,2,0:T(8,128)(2,1)} %bitcast.34) | data formatting | bytes 2621440 | tf_op jit(solution)/shard_map/reshape | solution.py:98
  325.1 14.2 %reduce.21 = bf16[2560,256]{1,0:T(8,128)(2,1)} reduce(bf16[2560,1,1,1,256]{4,3,2,1,0:T(2,128)(2,1)S(1)} %bitcast.168, bf16[]{:T(256)} %broadcast.133), dimensions={1,2,3}, to_apply=%bitcast.116.reduce_sub_computation | reduce | bytes 2621442
  339.3 4.2 %reshape.201 = bf16[16,2,20480]{2,1,0:T(2,128)(2,1)} reshape(bf16[2560,256]{1,0:T(8,128)(2,1)} %reduce.21) | data formatting | bytes 2621440
  343.5 7.2 %all-to-all-start.4 = ((bf16[16,2,20480]{2,1,0:T(2,128)(2,1)}), bf16[16,2,20480]{2,1,0:T(2,128)(2,1)}, u32[]{:S(2)}, u32[]{:S(2)}) async-start(bf16[16,2,20480]{2,1,0:T(2,128)(2,1)} %reshape.201), calls=%async_computation.4 | async-start | bytes 2621440 | tf_op jit(solution)/shard_map/all_to_all | solution.py:128
  352.6 4.1 %reshape.206 = bf16[2560,1,1,1,128]{4,3,2,1,0:T(2,128)(2,1)S(1)} reshape(bf16[16,2,10240]{2,1,0:T(2,128)(2,1)} %all-to-all-done.6) | data formatting | bytes 1310720
  357.9 10.8 %all-to-all-done.4 = bf16[16,2,20480]{2,1,0:T(2,128)(2,1)} async-done(((bf16[16,2,20480]{2,1,0:T(2,128)(2,1)}), bf16[16,2,20480]{2,1,0:T(2,128)(2,1)}, u32[]{:S(2)}, u32[]{:S(2)}) %all-to-all-start.4) | async-done | bytes 1310752 | tf_op jit(solution)/shard_map/all_to_all | solution.py:128
  368.7 4.5 %reshape.202 = bf16[2560,1,1,1,256]{4,3,2,1,0:T(2,128)(2,1)S(1)} reshape(bf16[16,2,20480]{2,1,0:T(2,128)(2,1)} %all-to-all-done.4) | data formatting | bytes 2621440
  (255 shorter events, 170.9 us)
Async XLA Ops:
  0.6 9.2 %copy-start.3 = (bf16[1,160,16,128]{3,2,1,0:T(8,128)(2,1)S(1)}, bf16[1,160,16,128]{3,2,1,0:T(8,128)(2,1)}, u32[]{:S(2)}) copy-start(bf16[1,160,16,128]{3,2,1,0:T(8,128)(2,1)} %param.8) | copy-start | bytes 1966084
  2.8 19.9 %all-to-all-start = ((bf16[1,160,16,1,128]{4,1,3,0,2:T(8,128)(2,1)}), bf16[1,160,16,1,128]{4,1,3,0,2:T(8,128)(2,1)S(1)}, u32[]{:S(2)}, u32[]{:S(2)}) async-start(bf16[1,160,16,1,128]{4,1,3,0,2:T(8,128)(2,1)} %bitcast.135), calls=%async_computation | async-start | bytes 1310720 | tf_op jit(solution)/shard_map/all_to_all | solution.py:122
  22.7 15.2 %all-to-all-start.2 = ((bf16[1,160,16,1,128]{4,1,3,0,2:T(8,128)(2,1)}), bf16[1,160,16,1,128]{4,1,3,0,2:T(8,128)(2,1)S(1)}, u32[]{:S(2)}, u32[]{:S(2)}) async-start(bf16[1,160,16,1,128]{4,1,3,0,2:T(8,128)(2,1)} %bitcast.134), calls=%async_computation.2 | async-start | bytes 1310720 | tf_op jit(solution)/shard_map/all_to_all | solution.py:123
  26.3 15.5 %collective-permute-start = (bf16[1,160,32,128]{3,2,1,0:T(8,128)(2,1)}, bf16[1,160,32,128]{3,2,1,0:T(8,128)(2,1)}, u32[]{:S(2)}, u32[]{:S(2)}) collective-permute-start(bf16[1,160,32,128]{3,2,1,0:T(8,128)(2,1)} %param.9), channel_id=1, source_target_pairs={{0,240},{16,0},{32,16},{48,32},{64,48},{80,64},{96,80},{112,96},{1... | collective-permute-start | bytes 3932168 | tf_op jit(solution)/shard_map/ppermute | solution.py:17
  38.0 3.7 copy-start.1
  38.0 21.5 %all-to-all-start.1 = ((bf16[1,160,16,1,256]{4,1,3,0,2:T(8,128)(2,1)}), bf16[1,160,16,1,256]{4,1,3,0,2:T(8,128)(2,1)S(1)}, u32[]{:S(2)}, u32[]{:S(2)}) async-start(bf16[1,160,16,1,256]{4,1,3,0,2:T(8,128)(2,1)} %copy.73), calls=%async_computation.1 | async-start | bytes 2621440 | tf_op jit(solution)/shard_map/all_to_all | solution.py:121
  59.4 23.0 %all-to-all-start.3 = ((bf16[1,160,16,1,256]{4,1,3,0,2:T(8,128)(2,1)}), bf16[1,160,16,1,256]{4,1,3,0,2:T(8,128)(2,1)S(1)}, u32[]{:S(2)}, u32[]{:S(2)}) async-start(bf16[1,160,16,1,256]{4,1,3,0,2:T(8,128)(2,1)} %copy.75), calls=%async_computation.3 | async-start | bytes 2621440 | tf_op jit(solution)/shard_map/all_to_all | solution.py:124
  63.3 1.3 copy-start.2
  91.1 3.2 copy-start
  107.8 3.1 copy-start
  124.5 3.1 copy-start
  141.2 3.1 copy-start
  157.9 3.2 copy-start
  174.6 3.2 copy-start
  191.3 3.2 copy-start
  208.0 3.2 copy-start
  224.7 3.1 copy-start
  241.4 3.1 copy-start
  282.8 29.6 %all-to-all-start.5 = ((bf16[16,2,10240]{2,1,0:T(2,128)(2,1)}), bf16[16,2,10240]{2,1,0:T(2,128)(2,1)S(1)}, u32[]{:S(2)}, u32[]{:S(2)}) async-start(bf16[16,2,10240]{2,1,0:T(2,128)(2,1)} %reshape.203), calls=%async_computation.5 | async-start | bytes 1310720 | tf_op jit(solution)/shard_map/all_to_all | solution.py:129
  312.4 31.1 %all-to-all-start.6 = ((bf16[16,2,10240]{2,1,0:T(2,128)(2,1)}), bf16[16,2,10240]{2,1,0:T(2,128)(2,1)}, u32[]{:S(2)}, u32[]{:S(2)}) async-start(bf16[16,2,10240]{2,1,0:T(2,128)(2,1)} %reshape.205), calls=%async_computation.6 | async-start | bytes 1310720 | tf_op jit(solution)/shard_map/all_to_all | solution.py:130
  343.5 25.1 %all-to-all-start.4 = ((bf16[16,2,20480]{2,1,0:T(2,128)(2,1)}), bf16[16,2,20480]{2,1,0:T(2,128)(2,1)}, u32[]{:S(2)}, u32[]{:S(2)}) async-start(bf16[16,2,20480]{2,1,0:T(2,128)(2,1)} %reshape.201), calls=%async_computation.4 | async-start | bytes 2621440 | tf_op jit(solution)/shard_map/all_to_all | solution.py:128
where the time goes:
time: 379 us; the launch traced here: 375 us
  local copies, waits for them, and re-layouts  134 us (35%)
  matrix products  80.9 us (21%)
  other arithmetic  62.4 us (16%)
  waiting for transfers between devices  59.9 us (16%)
  starting transfers between devices  36.3 us (10%)
    unnamed x3, other arithmetic  42.8 us
    dot_general x10, matrix products, band_terms(): jnp.einsum('ngbk,bngd->knd', probs_half, grad_block, preferred_element_ty...  23.9 us
    unnamed x20, local copies, waits for them, and re-layouts  22 us
    dot_general x10, matrix products, band_terms(): jnp.einsum('ngbk,knd->bngd', grad_scores, key_block, preferred_element_ty...  20.1 us
    dot_general x10, matrix products, band_terms(): jnp.einsum('bngd,knd->ngbk', grad_block, value_block, preferred_element_t...  16.2 us
    all_to_all x1, waiting for transfers between devices, body(): lax.all_to_all(packed_grads, 'ctx', split_axis=2, concat_axis=1, tiled=True)  15.5 us
    dot_general x10, matrix products, band_terms(): jnp.einsum('bngd,knd->ngbk', query_block, key_block, preferred_element_ty...  15 us
    dynamic_update_slice x20, local copies, waits for them, and re-layouts, one_block(): lax.dynamic_update_slice_in_dim(grad_value_acc, old_values + terms[2], fi...  14 us
  transfers between devices with their start and end apart: 8, of which 6 were waited for; matrix products, arithmetic and copies ran while one was open for 18% of the time, Pallas kernels for 0%

commit v1 on v0

v1 whole, which is shorter than its diff:
```python
import functools
import math

import jax
import jax.numpy as jnp
from jax import lax
from jax.experimental import pallas as pl
from jax.experimental.pallas import tpu as pltpu
from jax.sharding import PartitionSpec as P

MESH = pl.DeviceIdType.MESH
WINDOW = 1024
BLOCK = 128
BIG = 1e30
query_scale = 168.0 ** (-0.5)
exponent_scale = query_scale * math.log2(math.e)

F32 = jnp.float32
BF16 = jnp.bfloat16


def contract(left, right, dims):
    return lax.dot_general(left, right, (dims, ((), ())), preferred_element_type=F32)


def kernel(
    sections,
    members,
    q_hbm,
    k_hbm,
    v_hbm,
    g_hbm,
    dq_hbm,
    dk_hbm,
    dv_hbm,
    q_all,
    k_all,
    v_all,
    g_all,
    k_cols,
    weights,
    grad_probs,
    half_probs,
    grad_scores,
    norms,
    dk_sum,
    dv_sum,
    dq_all,
    dk_all,
    dv_all,
    in_send,
    in_recv,
    out_send,
    out_recv,
):
    section = lax.axis_index("section")
    me = lax.axis_index("ctx")
    side = math.isqrt(members)
    my_x, my_y = me // side, me % side
    rows = q_hbm.shape[0]
    length = rows * members
    per_group = q_hbm.shape[2]
    blocks = length // BLOCK
    tiles = WINDOW // BLOCK + 1
    span = WINDOW + BLOCK
    lanes = per_group * BLOCK
    behind = (section + sections - 1) % sections
    ahead = (section + 1) % sections

    def peer(step):
        x = (my_x + step // side) % side
        y = (my_y + step % side) % side
        return x * side + y

    barrier = pltpu.get_barrier_semaphore()

    def greet(step, carry):
        pl.semaphore_signal(
            barrier, inc=1, device_id=(ahead, peer(step)), device_id_type=MESH
        )

        @pl.when(step > 0)
        def _():
            pl.semaphore_signal(
                barrier, inc=1, device_id=(section, peer(step)), device_id_type=MESH
            )

        return carry

    lax.fori_loop(0, members, greet, 0)
    pl.semaphore_wait(barrier, 2 * members - 1)

    def place(buffer, who, pad):
        return buffer.at[pl.ds(pad + who * rows, rows)]

    def inbound(number, source, buffer, pad):
        def send(step, carry):
            who = peer(step)

            @pl.when(step == 0)
            def _():
                pltpu.make_async_copy(
                    source(who), place(buffer, me, pad), in_recv.at[number]
                ).start()

            @pl.when(step > 0)
            def _():
                pltpu.make_async_remote_copy(
                    src_ref=source(who),
                    dst_ref=place(buffer, me, pad),
                    send_sem=in_send.at[number],
                    recv_sem=in_recv.at[number],
                    device_id=(section, who),
                    device_id_type=MESH,
                ).start()

            return carry

        lax.fori_loop(0, members, send, 0)

    inbound(0, lambda who: k_hbm.at[who], k_all, WINDOW)
    inbound(1, lambda who: q_hbm.at[:, who], q_all, 0)
    inbound(2, lambda who: v_hbm.at[who], v_all, WINDOW)

    def send_grad(step, carry):
        who = peer(step)
        pltpu.make_async_remote_copy(
            src_ref=g_hbm.at[:, who],
            dst_ref=place(g_all, me, 0),
            send_sem=in_send.at[3],
            recv_sem=in_recv.at[3],
            device_id=(behind, who),
            device_id_type=MESH,
        ).start()
        return carry

    lax.fori_loop(0, members, send_grad, 0)

    def await_bytes(view, semaphore):
        pltpu.make_async_copy(view, view, semaphore).wait()

    k_all[0:WINDOW, :] = jnp.zeros((WINDOW, k_all.shape[1]), BF16)
    v_all[0:WINDOW, :] = jnp.zeros((WINDOW, v_all.shape[1]), BF16)
    dk_sum[...] = jnp.zeros(dk_sum.shape, F32)
    dv_sum[...] = jnp.zeros(dv_sum.shape, F32)

    q_rows = q_all.reshape(length * per_group, q_all.shape[2])
    g_rows = g_all.reshape(length * per_group, g_all.shape[2])
    dq_rows = dq_all.reshape(length * per_group, dq_all.shape[2])

    await_bytes(k_all.at[pl.ds(WINDOW, length)], in_recv.at[0])

    def turn(tile, carry):
        first = pl.multiple_of(tile * BLOCK, BLOCK)
        k_cols[:, pl.ds(first, BLOCK)] = k_all[pl.ds(first, BLOCK), :].T
        return carry

    lax.fori_loop(0, (length + WINDOW) // BLOCK, turn, 0)
    await_bytes(q_all, in_recv.at[1])

    def weigh(block, carry):
        first = pl.multiple_of(block * BLOCK, BLOCK)
        query = q_rows[pl.ds(pl.multiple_of(block * lanes, lanes), lanes), :]
        scores = contract(k_all[pl.ds(first, span), :], query, ((1,), (1,)))
        key_place = lax.broadcasted_iota(jnp.int32, (BLOCK, lanes), 0)
        query_place = lax.broadcasted_iota(jnp.int32, (BLOCK, lanes), 1) // per_group
        tops = []
        for tile in range(tiles):
            part = scores[tile * BLOCK : (tile + 1) * BLOCK, :]
            if tile == 0:
                part = jnp.where(key_place > query_place, part, -BIG)
            if tile == tiles - 1:
                part = jnp.where(key_place <= query_place, part, -BIG)
            weights[block, tile * BLOCK : (tile + 1) * BLOCK, :] = part
            top = jnp.max(part, axis=0, keepdims=True)
            tops.append(jnp.where(tile + block >= tiles - 1, top, -BIG))
        row_max = functools.reduce(jnp.maximum, tops)
        total = jnp.zeros((1, lanes), F32)
        for tile in range(tiles):
            level = jnp.where(tile + block >= tiles - 1, row_max, BIG)
            part = weights[block, tile * BLOCK : (tile + 1) * BLOCK, :]
            part = jnp.exp2((part - level) * exponent_scale)
            weights[block, tile * BLOCK : (tile + 1) * BLOCK, :] = part
            total = total + jnp.sum(part, axis=0, keepdims=True)
        norms[block] = 1.0 / total
        return carry

    lax.fori_loop(0, blocks, weigh, 0)

    await_bytes(v_all.at[pl.ds(WINDOW, length)], in_recv.at[2])
    await_bytes(g_all, in_recv.at[3])

    groups = 4
    group_blocks = blocks // groups
    group_members = members // groups

    def home(step):
        return (my_x + 1 + step // group_blocks) % groups

    def send_query_grads(step):
        who = home(step) * group_members + step % group_blocks - 1
        source = dq_all.at[pl.ds(who * rows, rows)]

        @pl.when(who == me)
        def _():
            pltpu.make_async_copy(source, dq_hbm.at[:, me], out_recv.at[0]).start()

        @pl.when(who != me)
        def _():
            pltpu.make_async_remote_copy(
                src_ref=source,
                dst_ref=dq_hbm.at[:, me],
                send_sem=out_send.at[0],
                recv_sem=out_recv.at[0],
                device_id=(section, who),
                device_id_type=MESH,
            ).start()

    def grads(step, carry):
        block = home(step) * group_blocks + step % group_blocks
        first = pl.multiple_of(block * BLOCK, BLOCK)
        window = pl.ds(first, span)
        band = pl.ds(pl.multiple_of(block * lanes, lanes), lanes)
        incoming = g_rows[band, :]
        norm = norms[block]
        products = contract(v_all[window, :], incoming, ((1,), (1,)))
        row_dot = jnp.zeros((1, lanes), F32)
        for tile in range(tiles):
            cut = slice(tile * BLOCK, (tile + 1) * BLOCK)
            part = products[cut, :]
            probs = weights[block, cut, :] * norm
            half_probs[cut, :] = probs.astype(BF16)
            grad_probs[cut, :] = part
            row_dot = row_dot + jnp.sum(probs * part, axis=0, keepdims=True)
        for tile in range(tiles):
            cut = slice(tile * BLOCK, (tile + 1) * BLOCK)
            probs = weights[block, cut, :] * norm
            grad_scores[cut, :] = (probs * (grad_probs[cut, :] - row_dot)).astype(BF16)
        dv_sum[window, :] += contract(half_probs[...], incoming, ((1,), (0,)))
        dk_sum[window, :] += contract(grad_scores[...], q_rows[band, :], ((1,), (0,)))
        turned = contract(k_cols[:, window], grad_scores[...], ((1,), (0,)))
        dq_rows[band, :] = (turned * query_scale).T.astype(BF16)

        @pl.when((step > 0) & ((step + group_blocks - 1) % group_blocks > 0))
        def _():
            send_query_grads(step - 1)

        return carry

    lax.fori_loop(0, blocks, grads, 0)
    send_query_grads(blocks - 1)

    def finish(block, carry):
        here = pl.ds(pl.multiple_of(block * BLOCK, BLOCK), BLOCK)
        there = pl.ds(pl.multiple_of(WINDOW + block * BLOCK, BLOCK), BLOCK)
        dk_all[here, :] = (dk_sum[there, :] * query_scale).astype(BF16)
        dv_all[here, :] = dv_sum[there, :].astype(BF16)
        return carry

    lax.fori_loop(0, blocks, finish, 0)

    def outbound(number, source, target):
        def send(step, carry):
            who = peer(step)
            mine = source.at[pl.ds(who * rows, rows)]

            @pl.when(step == 0)
            def _():
                pltpu.make_async_copy(mine, target.at[me], out_recv.at[number]).start()

            @pl.when(step > 0)
            def _():
                pltpu.make_async_remote_copy(
                    src_ref=mine,
                    dst_ref=target.at[me],
                    send_sem=out_send.at[number],
                    recv_sem=out_recv.at[number],
                    device_id=(section, who),
                    device_id_type=MESH,
                ).start()

            return carry

        lax.fori_loop(0, members, send, 0)

    outbound(1, dv_all, dv_hbm)
    outbound(2, dk_all, dk_hbm)

    others = pl.ds(0, length - rows)
    await_bytes(k_all.at[others], in_send.at[0])
    await_bytes(q_all.at[others], in_send.at[1])
    await_bytes(v_all.at[others], in_send.at[2])
    await_bytes(g_all, in_send.at[3])
    await_bytes(dq_all.at[others], out_send.at[0])
    await_bytes(dv_all.at[others], out_send.at[1])
    await_bytes(dk_all.at[others], out_send.at[2])
    await_bytes(dq_all, out_recv.at[0])
    await_bytes(dv_all, out_recv.at[1])
    await_bytes(dk_all, out_recv.at[2])


def solution(mesh):
    sections, members = mesh.shape["section"], mesh.shape["ctx"]

    def body(queries, key_rows, stored_value_rows, grad_out):
        _, rows, heads, width = queries.shape
        groups = key_rows.shape[2]
        per_group = heads // groups
        length = rows * members
        blocks = length // BLOCK
        span = WINDOW + BLOCK
        lanes = per_group * BLOCK
        by_group = (rows, groups, per_group, width)
        anywhere = pl.BlockSpec(memory_space=pl.ANY)
        dq, dk, dv = pl.pallas_call(
            functools.partial(kernel, sections, members),
            out_shape=(
                jax.ShapeDtypeStruct(by_group, BF16),
                jax.ShapeDtypeStruct((groups, rows, width), BF16),
                jax.ShapeDtypeStruct((groups, rows, width), BF16),
            ),
            in_specs=[anywhere] * 4,
            out_specs=(anywhere,) * 3,
            scratch_shapes=[
                pltpu.VMEM((length, per_group, width), BF16),
                pltpu.VMEM((length + WINDOW, width), BF16),
                pltpu.VMEM((length + WINDOW, width), BF16),
                pltpu.VMEM((length, per_group, width), BF16),
                pltpu.VMEM((width, length + WINDOW), BF16),
                pltpu.VMEM((blocks, span, lanes), F32),
                pltpu.VMEM((span, lanes), F32),
                pltpu.VMEM((span, lanes), BF16),
                pltpu.VMEM((span, lanes), BF16),
                pltpu.VMEM((blocks, 1, lanes), F32),
                pltpu.VMEM((length + WINDOW, width), F32),
                pltpu.VMEM((length + WINDOW, width), F32),
                pltpu.VMEM((length, per_group, width), BF16),
                pltpu.VMEM((length, width), BF16),
                pltpu.VMEM((length, width), BF16),
                pltpu.SemaphoreType.DMA((4,)),
                pltpu.SemaphoreType.DMA((4,)),
                pltpu.SemaphoreType.DMA((3,)),
                pltpu.SemaphoreType.DMA((3,)),
            ],
            compiler_params=pltpu.CompilerParams(
                collective_id=0, has_side_effects=True, vmem_limit_bytes=60 << 20
            ),
            name="relay_attention_backward",
        )(
            queries.reshape(by_group),
            key_rows[0].transpose(1, 0, 2),
            stored_value_rows[0].transpose(1, 0, 2),
            grad_out.reshape(by_group),
        )
        return (
            dq.reshape(1, rows, heads, width),
            dk.transpose(1, 0, 2)[None],
            dv.transpose(1, 0, 2)[None],
        )

    spec = P("section", "ctx", None, None)
    return jax.shard_map(
        body, mesh=mesh, in_specs=(spec,) * 4, out_specs=(spec,) * 3, check_vma=False
    )
```

time: 379 us -> 102 us (0.27)
  local copies, waits for them, and re-layouts: 134 us -> 7.15 us
  Pallas kernels: 0 us -> 92.9 us
  matrix products: 80.9 us -> 0 us
  other arithmetic: 62.4 us -> 0 us
  waiting for transfers between devices: 59.9 us -> 0 us
  starting transfers between devices: 36.3 us -> 0 us
    pallas_call x0 -> x1, Pallas kernels: none -> 92.9 us  [body(): pl.pallas_call(functools.partial(kernel, sections, members), out_shape=(j...]
    dot_general x50 -> x0, matrix products: 80.9 us -> none  [the longest x10 23.9 us: band_terms(): jnp.einsum('ngbk,bngd->knd', probs_half, grad_block, preferred_element_ty...]
    all_to_all x7 -> x0, waiting for transfers between devices: 59.8 us -> none  [the longest x1 15.5 us: body(): lax.all_to_all(packed_grads, 'ctx', split_axis=2, concat_axis=1, tiled=True)]
    dynamic_slice x60 -> x0, local copies, waits for them, and re-layouts: 48.7 us -> none  [the longest x20 13.7 us: one_block(): old_keys = lax.dynamic_slice_in_dim(key_gradient_total, first_row, span, 0)]
    unnamed x3 -> x0, other arithmetic: 42.8 us -> none
    reshape x9 -> x0, local copies, waits for them, and re-layouts: 37.5 us -> none  [the longest x2 12.4 us: heads_grads(): finals[1][WINDOW:].astype(jnp.bfloat16)]
    all_to_all x7 -> x0, starting transfers between devices: 36.2 us -> none  [the longest x1 7.23 us: body(): lax.all_to_all(results[0], 'ctx', split_axis=1, concat_axis=2, tiled=True)]
    unnamed x20 -> x7, local copies, waits for them, and re-layouts: 22 us -> 4.47 us
  transfers between devices with their start and end apart: 8 -> 0, of which waited for: 6 -> 0; matrix products, arithmetic and copies ran while one was open for 18% -> 0% of each run, Pallas kernels for 0% -> 0%
where the time goes in v1:
time: 102 us; the launch traced here: 101 us
  Pallas kernels  92.9 us (91%)
  local copies, waits for them, and re-layouts  7.15 us (7%)
    pallas_call x1, Pallas kernels, body(): pl.pallas_call(functools.partial(kernel, sections, members), out_shape=(j...  92.9 us
    unnamed x7, local copies, waits for them, and re-layouts  4.47 us
    transpose x1, local copies, waits for them, and re-layouts, body(): stored_value_rows[0].transpose(1, 0, 2)  2.67 us

profile of v1, /device:TPU:96, one launch (start us, length us, event | category | flops | bytes accessed | tf_op | source)
XLA Modules:
  0.0 100.7 jit_solution(13586830290490879186)
XLA Ops:
  0.6 2.7 %copy_bitcast_fusion = (bf16[16,160,128]{2,1,0:T(8,128)(2,1)}, bf16[16,160,128]{2,1,0:T(8,128)(2,1)}) fusion(bf16[1,160,16,128]{3,2,1,0:T(8,128)(2,1)} %param.6, bf16[1,160,16,128]{3,2,1,0:T(8,128)(2,1)} %param.5), kind=kLoop, calls=%fused_computation | loop fusion | bytes 2621440 | tf_op jit(solution)/shard_map/transpose | solution.py:352
  3.3 92.9 %relay_attention_backward.1 = (bf16[160,16,2,128]{3,2,1,0:T(2,128)(2,1)}, bf16[16,160,128]{2,1,0:T(8,128)(2,1)}, bf16[16,160,128]{2,1,0:T(8,128)(2,1)}) custom-call(bf16[160,16,2,128]{3,2,1,0:T(2,128)(2,1)} %bitcast.18, bf16[16,160,128]{2,1,0:T(8,128)(2,1)} %get-tuple-element.13.k_hbm, bf16[16,160,128]{2,1,0:T(8,128)(2,1)} %get-tuple-element.12.v_hbm, ...), custom_call_target="tpu_custom_call" | custom-call | tf_op jit(solution)/shard_map/relay_attention_backward/pallas_call | solution.py:315
  96.2 0.0 copy-start.1
  96.2 0.0 copy-start
  96.2 2.3 %copy.9 = bf16[1,160,16,128]{3,2,1,0:T(8,128)(2,1)} copy(bf16[1,160,16,128]{3,1,2,0:T(8,128)(2,1)} %bitcast.21) | data formatting | bytes 1310720
  98.5 0.0 copy-done.1
  98.5 1.1 %copy.10 = bf16[1,160,16,128]{3,2,1,0:T(8,128)(2,1)} copy(bf16[1,160,16,128]{3,1,2,0:T(8,128)(2,1)S(1)} %bitcast.20) | data formatting | bytes 1310720
  99.6 0.0 copy-done
  99.6 1.1 %copy.14 = bf16[1,160,32,128]{3,2,1,0:T(8,128)(2,1)} copy(bf16[1,160,32,128]{3,2,1,0:T(8,128)(2,1)S(1)} %bitcast.17) | data formatting | bytes 2621440
Async XLA Ops:
  96.2 2.3 %copy-start.1 = (bf16[16,160,128]{2,1,0:T(8,128)(2,1)S(1)}, bf16[16,160,128]{2,1,0:T(8,128)(2,1)}, u32[]{:S(2)}) copy-start(bf16[16,160,128]{2,1,0:T(8,128)(2,1)} %get-tuple-element.8) | copy-start | bytes 1966084
  96.2 3.4 %copy-start = (bf16[160,16,2,128]{3,2,1,0:T(2,128)(2,1)S(1)}, bf16[160,16,2,128]{3,2,1,0:T(2,128)(2,1)}, u32[]{:S(2)}) copy-start(bf16[160,16,2,128]{3,2,1,0:T(2,128)(2,1)} %get-tuple-element.6) | copy-start | bytes 3932164

commit v2 on v1

v2 whole, which is shorter than its diff:
```python
import functools
import math

import jax
import jax.numpy as jnp
from jax import lax
from jax.experimental import pallas as pl
from jax.experimental.pallas import tpu as pltpu
from jax.sharding import PartitionSpec as P

MESH = pl.DeviceIdType.MESH
WINDOW = 1024
BLOCK = 128
CHUNK = 32
BIG = 1e30
query_scale = 168.0 ** (-0.5)
exponent_scale = query_scale * math.log2(math.e)

F32 = jnp.float32
BF16 = jnp.bfloat16


def contract(left, right, dims):
    return lax.dot_general(left, right, (dims, ((), ())), preferred_element_type=F32)


def kernel(
    sections,
    members,
    q_hbm,
    k_hbm,
    v_hbm,
    g_hbm,
    dq_out,
    dk_out,
    dv_out,
    q_all,
    k_all,
    v_all,
    g_all,
    k_cols,
    weights,
    norms,
    grad_probs,
    next_probs,
    grad_scores,
    dk_sum,
    dv_sum,
    dq_all,
    dk_all,
    dv_all,
    q_raw,
    k_raw,
    v_raw,
    g_raw,
    q_ready,
    k_ready,
    v_ready,
    g_ready,
    dq_back,
    dk_back,
    dv_back,
    wide,
    load_sem,
    in_send,
    in_recv,
    out_send,
    out_recv,
):
    section = lax.axis_index("section")
    me = lax.axis_index("ctx")
    side = math.isqrt(members)
    my_x, my_y = me // side, me % side
    rows = q_hbm.shape[0]
    length = rows * members
    heads, groups = q_hbm.shape[1], k_hbm.shape[1]
    per_group = heads // groups
    blocks = length // BLOCK
    tiles = WINDOW // BLOCK + 1
    span = WINDOW + BLOCK
    lanes = per_group * BLOCK
    behind = (section + sections - 1) % sections
    ahead = (section + 1) % sections

    def peer(step):
        x = (my_x + step) % side
        y = (my_y + step // side + step) % side
        return x * side + y

    loads = [
        pltpu.make_async_copy(source, raw, load_sem.at[number])
        for number, (source, raw) in enumerate(
            ((k_hbm, k_raw), (q_hbm, q_raw), (v_hbm, v_raw), (g_hbm, g_raw))
        )
    ]
    for load in loads:
        load.start()

    barrier = pltpu.get_barrier_semaphore()

    def greet(step, carry):
        pl.semaphore_signal(
            barrier, inc=1, device_id=(ahead, peer(step)), device_id_type=MESH
        )

        @pl.when(step > 0)
        def _():
            pl.semaphore_signal(
                barrier, inc=1, device_id=(section, peer(step)), device_id_type=MESH
            )

        return carry

    lax.fori_loop(0, members, greet, 0)

    def by_group(raw, ready):
        count = raw.shape[1]
        each = count // groups
        flat = raw.reshape(rows * count, raw.shape[2])

        def one(chunk, carry):
            here = pl.ds(pl.multiple_of(chunk * CHUNK * count, CHUNK), CHUNK * count)
            wide[0 : CHUNK * count, :] = flat[here, :].astype(F32)
            for head in range(count):
                first = (chunk * each + head % each) * CHUNK
                ready[head // each, pl.ds(pl.multiple_of(first, CHUNK), CHUNK), :] = (
                    wide[pl.ds(head, CHUNK, stride=count), :].astype(BF16)
                )
            return carry

        lax.fori_loop(0, rows // CHUNK, one, 0)

    def by_row(back, out):
        count = out.shape[1]
        each = count // groups
        flat = out.reshape(rows * count, out.shape[2])

        def one(chunk, carry):
            for head in range(count):
                first = (chunk * each + head % each) * CHUNK
                wide[pl.ds(head, CHUNK, stride=count), :] = back[
                    head // each, pl.ds(pl.multiple_of(first, CHUNK), CHUNK), :
                ].astype(F32)
            here = pl.ds(pl.multiple_of(chunk * CHUNK * count, CHUNK), CHUNK * count)
            flat[here, :] = wide[0 : CHUNK * count, :].astype(BF16)
            return carry

        lax.fori_loop(0, rows // CHUNK, one, 0)

    loads[0].wait()
    by_group(k_raw, k_ready)
    pl.semaphore_wait(barrier, 2 * members - 1)

    def inbound(number, ready, buffer, pad, target_section):
        size = ready.shape[1]
        there = buffer.at[pl.ds(pad + me * size, size)]

        def send(step, carry):
            who = peer(step)
            near = (step == 0) & (target_section == section)

            @pl.when(near)
            def _():
                pltpu.make_async_copy(
                    ready.at[who], there, in_recv.at[number]
                ).start()

            @pl.when(jnp.logical_not(near))
            def _():
                pltpu.make_async_remote_copy(
                    src_ref=ready.at[who],
                    dst_ref=there,
                    send_sem=in_send.at[number],
                    recv_sem=in_recv.at[number],
                    device_id=(target_section, who),
                    device_id_type=MESH,
                ).start()

            return carry

        lax.fori_loop(0, members, send, 0)

    inbound(0, k_ready, k_all, WINDOW, section)
    loads[1].wait()
    by_group(q_raw, q_ready)
    inbound(1, q_ready, q_all, 0, section)
    loads[2].wait()
    by_group(v_raw, v_ready)
    inbound(2, v_ready, v_all, WINDOW, section)
    loads[3].wait()
    by_group(g_raw, g_ready)
    inbound(3, g_ready, g_all, 0, behind)

    def await_bytes(view, semaphore):
        pltpu.make_async_copy(view, view, semaphore).wait()

    k_all[0:WINDOW, :] = jnp.zeros((WINDOW, k_all.shape[1]), BF16)
    v_all[0:WINDOW, :] = jnp.zeros((WINDOW, v_all.shape[1]), BF16)
    dk_sum[...] = jnp.zeros(dk_sum.shape, F32)
    dv_sum[...] = jnp.zeros(dv_sum.shape, F32)

    await_bytes(k_all.at[pl.ds(WINDOW, length)], in_recv.at[0])

    def turn(tile, carry):
        first = pl.multiple_of(tile * BLOCK, BLOCK)
        k_cols[:, pl.ds(first, BLOCK)] = k_all[pl.ds(first, BLOCK), :].T
        return carry

    lax.fori_loop(0, (length + WINDOW) // BLOCK, turn, 0)

    await_bytes(q_all, in_recv.at[1])

    def weigh(block, carry):
        first = pl.multiple_of(block * BLOCK, BLOCK)
        query = q_all[pl.ds(pl.multiple_of(block * lanes, lanes), lanes), :]
        scores = contract(k_all[pl.ds(first, span), :], query, ((1,), (1,)))
        key_place = lax.broadcasted_iota(jnp.int32, (BLOCK, lanes), 0)
        lane = lax.broadcasted_iota(jnp.int32, (BLOCK, lanes), 1)
        query_place = lane // (CHUNK * per_group) * CHUNK + lane % CHUNK
        tops = []
        for tile in range(tiles):
            part = scores[tile * BLOCK : (tile + 1) * BLOCK, :]
            if tile == 0:
                part = jnp.where(key_place > query_place, part, -BIG)
            if tile == tiles - 1:
                part = jnp.where(key_place <= query_place, part, -BIG)
            weights[block, tile * BLOCK : (tile + 1) * BLOCK, :] = part
            top = jnp.max(part, axis=0, keepdims=True)
            tops.append(jnp.where(tile + block >= tiles - 1, top, -BIG))
        row_max = functools.reduce(jnp.maximum, tops)
        total = jnp.zeros((1, lanes), F32)
        for tile in range(tiles):
            level = jnp.where(tile + block >= tiles - 1, row_max, BIG)
            part = weights[block, tile * BLOCK : (tile + 1) * BLOCK, :]
            part = jnp.exp2((part - level) * exponent_scale)
            weights[block, tile * BLOCK : (tile + 1) * BLOCK, :] = part
            total = total + jnp.sum(part, axis=0, keepdims=True)
        norms[block] = 1.0 / total
        return carry

    lax.fori_loop(0, blocks, weigh, 0)

    await_bytes(v_all.at[pl.ds(WINDOW, length)], in_recv.at[2])
    await_bytes(g_all, in_recv.at[3])

    group_blocks = blocks // side

    def block_of(step):
        row = (my_x + my_y + 1 + step // group_blocks) % side
        return row * group_blocks + (my_y + step) % group_blocks

    def send_query_grads(who):
        source = dq_all.at[pl.ds(who * rows * per_group, rows * per_group)]

        @pl.when(who == me)
        def _():
            pltpu.make_async_copy(source, dq_back.at[me], out_recv.at[0]).start()

        @pl.when(who != me)
        def _():
            pltpu.make_async_remote_copy(
                src_ref=source,
                dst_ref=dq_back.at[me],
                send_sem=out_send.at[0],
                recv_sem=out_recv.at[0],
                device_id=(section, who),
                device_id_type=MESH,
            ).start()

    def release(step):
        turn = step % group_blocks
        place = (my_y + step) % group_blocks
        row = block_of(step) // group_blocks * side

        def done(other):
            return (other + group_blocks - my_y) % group_blocks < turn

        @pl.when((place > 0) & done(place + group_blocks - 1))
        def _():
            send_query_grads(row + place - 1)

        @pl.when((place < side) & done(place + 1))
        def _():
            send_query_grads(row + place)

    def places(step):
        block = block_of(step)
        window = pl.ds(pl.multiple_of(block * BLOCK, BLOCK), span)
        return block, window, pl.ds(pl.multiple_of(block * lanes, lanes), lanes)

    tile_cuts = [slice(tile * BLOCK, (tile + 1) * BLOCK) for tile in range(tiles)]

    def look_ahead(step, products_out):
        block, window, band = places(step)
        products = contract(v_all[window, :], g_all[band, :], ((1,), (1,)))
        row_dot = jnp.zeros((1, lanes), F32)
        for cut in tile_cuts:
            part = products[cut, :]
            products_out[cut, :] = part
            row_dot = row_dot + jnp.sum(
                weights[block, cut, :] * part, axis=0, keepdims=True
            )
            yield row_dot * norms[block]

    def grads(step, after, products_in, products_out, row_dot):
        block, window, band = places(step)
        norm = norms[block]
        ahead_dots = look_ahead(after, products_out)
        for cut in tile_cuts:
            next_dot = next(ahead_dots)
            grad_scores[cut, :] = (
                weights[block, cut, :] * ((products_in[cut, :] - row_dot) * norm)
            ).astype(BF16)
        dk_sum[window, :] += contract(grad_scores[...], q_all[band, :], ((1,), (0,)))
        turned = contract(k_cols[:, window], grad_scores[...], ((1,), (0,)))
        dq_all[band, :] = (turned * query_scale).T.astype(BF16)
        return next_dot

    def two_blocks(pair, row_dot):
        step = 2 * pair
        last = blocks - 1
        row_dot = grads(step, step + 1, grad_probs, next_probs, row_dot)
        row_dot = grads(
            step + 1, jnp.minimum(step + 2, last), next_probs, grad_probs, row_dot
        )

        @pl.when(pair > 0)
        def _():
            release(step - 1)

        release(step)
        return row_dot

    first_dot = list(look_ahead(0, grad_probs))[-1]
    lax.fori_loop(0, blocks // 2, two_blocks, first_dot)
    release(blocks - 1)

    def finish(total, result, scale):
        def one(block, carry):
            here = pl.ds(pl.multiple_of(block * BLOCK, BLOCK), BLOCK)
            there = pl.ds(pl.multiple_of(WINDOW + block * BLOCK, BLOCK), BLOCK)
            result[here, :] = (total[there, :] * scale).astype(BF16)
            return carry

        lax.fori_loop(0, blocks, one, 0)

    def outbound(number, source, target):
        def send(step, carry):
            who = peer(step)
            mine = source.at[pl.ds(who * rows, rows)]

            @pl.when(step == 0)
            def _():
                pltpu.make_async_copy(mine, target.at[me], out_recv.at[number]).start()

            @pl.when(step > 0)
            def _():
                pltpu.make_async_remote_copy(
                    src_ref=mine,
                    dst_ref=target.at[me],
                    send_sem=out_send.at[number],
                    recv_sem=out_recv.at[number],
                    device_id=(section, who),
                    device_id_type=MESH,
                ).start()

            return carry

        lax.fori_loop(0, members, send, 0)

    finish(dk_sum, dk_all, query_scale)
    outbound(2, dk_all, dk_back)

    def value_grads(block, carry):
        first = pl.multiple_of(block * BLOCK, BLOCK)
        band = pl.ds(pl.multiple_of(block * lanes, lanes), lanes)
        dv_sum[pl.ds(first, span), :] += contract(
            (weights[block] * norms[block]).astype(BF16),
            g_all[band, :],
            ((1,), (0,)),
        )
        return carry

    lax.fori_loop(0, blocks, value_grads, 0)
    finish(dv_sum, dv_all, 1.0)
    outbound(1, dv_all, dv_back)

    def others(buffer):
        size = buffer.shape[0] // members
        return buffer.at[pl.ds(0, size * (members - 1))]

    await_bytes(others(k_ready), in_send.at[0])
    await_bytes(others(q_ready), in_send.at[1])
    await_bytes(others(v_ready), in_send.at[2])
    await_bytes(g_ready, in_send.at[3])
    await_bytes(dq_back, out_recv.at[0])
    by_row(dq_back, dq_out)
    await_bytes(dk_back, out_recv.at[2])
    by_row(dk_back, dk_out)
    await_bytes(others(dq_all), out_send.at[0])
    await_bytes(others(dk_all), out_send.at[2])
    await_bytes(dv_back, out_recv.at[1])
    by_row(dv_back, dv_out)
    await_bytes(others(dv_all), out_send.at[1])


def solution(mesh):
    sections, members = mesh.shape["section"], mesh.shape["ctx"]

    def body(queries, key_rows, stored_value_rows, grad_out):
        _, rows, heads, width = queries.shape
        groups = key_rows.shape[2]
        per_group = heads // groups
        length = rows * members
        blocks = length // BLOCK
        span = WINDOW + BLOCK
        lanes = per_group * BLOCK
        outside = pl.BlockSpec(memory_space=pltpu.HBM)
        inside = pl.BlockSpec(memory_space=pltpu.VMEM)
        q_row, kv_row = (rows, heads, width), (rows, groups, width)
        q_sent = (groups, rows * per_group, width)
        kv_sent = (groups, rows, width)
        half = functools.partial(pltpu.VMEM, dtype=BF16)
        full = functools.partial(pltpu.VMEM, dtype=F32)
        dq, dk, dv = pl.pallas_call(
            functools.partial(kernel, sections, members),
            out_shape=tuple(
                jax.ShapeDtypeStruct(shape, BF16) for shape in (q_row, kv_row, kv_row)
            ),
            in_specs=[outside] * 4,
            out_specs=(inside,) * 3,
            scratch_shapes=[
                half((length * per_group, width)),
                half((length + WINDOW, width)),
                half((length + WINDOW, width)),
                half((length * per_group, width)),
                half((width, length + WINDOW)),
                full((blocks, span, lanes)),
                full((blocks, 1, lanes)),
                full((span, lanes)),
                full((span, lanes)),
                half((span, lanes)),
                full((length + WINDOW, width)),
                full((length + WINDOW, width)),
                half((length * per_group, width)),
                half((length, width)),
                half((length, width)),
                half(q_row),
                half(kv_row),
                half(kv_row),
                half(q_row),
                half(q_sent),
                half(kv_sent),
                half(kv_sent),
                half(q_sent),
                half(q_sent),
                half(kv_sent),
                half(kv_sent),
                full((CHUNK * heads, width)),
                pltpu.SemaphoreType.DMA((4,)),
                pltpu.SemaphoreType.DMA((4,)),
                pltpu.SemaphoreType.DMA((4,)),
                pltpu.SemaphoreType.DMA((3,)),
                pltpu.SemaphoreType.DMA((3,)),
            ],
            compiler_params=pltpu.CompilerParams(
                collective_id=0, has_side_effects=True, vmem_limit_bytes=51 << 20
            ),
            name="relay_attention_backward",
        )(
            *(
                pltpu.with_memory_space_constraint(array, pltpu.HBM)
                for array in (
                    queries[0],
                    key_rows[0],
                    stored_value_rows[0],
                    grad_out[0],
                )
            ),
        )
        return dq[None], dk[None], dv[None]

    spec = P("section", "ctx", None, None)
    return jax.shard_map(
        body, mesh=mesh, in_specs=(spec,) * 4, out_specs=(spec,) * 3, check_vma=False
    )
```

time: 102 us -> 97.2 us (0.953)
  local copies, waits for them, and re-layouts: 7.15 us -> 2.73 us
    transpose x1 -> x0, local copies, waits for them, and re-layouts: 2.67 us -> none  [body(): stored_value_rows[0].transpose(1, 0, 2)]
    unnamed x7 -> x3, local copies, waits for them, and re-layouts: 4.47 us -> 2.73 us
where the time goes in v2:
time: 97.2 us; the launch traced here: 95.9 us
  Pallas kernels  92.6 us (95%)
  local copies, waits for them, and re-layouts  2.73 us (3%)
    pallas_call x1, Pallas kernels, body(): pl.pallas_call(functools.partial(kernel, sections, members), out_shape=tu...  92.6 us
    unnamed x3, local copies, waits for them, and re-layouts  2.73 us

profile of v2, /device:TPU:96, one launch (start us, length us, event | category | flops | bytes accessed | tf_op | source)
XLA Modules:
  0.0 95.9 jit_solution(5070910643478400410)
XLA Ops:
  0.6 92.6 %relay_attention_backward.1 = (bf16[160,32,128]{2,1,0:T(8,128)(2,1)S(1)}, bf16[160,16,128]{2,1,0:T(8,128)(2,1)S(1)}, bf16[160,16,128]{2,1,0:T(8,128)(2,1)S(1)}) custom-call(bf16[160,32,128]{2,1,0:T(8,128)(2,1)} %bitcast.10, bf16[160,16,128]{2,1,0:T(8,128)(2,1)} %bitcast.12, bf16[160,16,128]{2,1,0:T(8,128)(2,1)} %bitcast.13, bf16[160,32,128]{2,1,0:T(8,128)(2,1)} %bitcast.11), custom_call_target="tpu_custom_call" | custom-call | tf_op jit(solution)/shard_map/relay_attention_backward/pallas_call | solution.py:425
  93.2 1.1 %copy.10 = bf16[1,160,32,128]{3,2,1,0:T(8,128)(2,1)} copy(bf16[1,160,32,128]{3,2,1,0:T(8,128)(2,1)S(1)} %bitcast.7) | data formatting | bytes 2621440
  94.3 0.8 copy.11
  95.1 0.8 copy.12

commit v3 on v2

--- a/solution.py
+++ b/solution.py
@@ -151,24 +151,26 @@
     by_group(k_raw, k_ready)
     pl.semaphore_wait(barrier, 2 * members - 1)
 
-    def inbound(number, ready, buffer, pad, target_section):
+    def inbound(number, ready, buffer, pad, target_section, parts):
         size = ready.shape[1]
-        there = buffer.at[pl.ds(pad + me * size, size)]
-
-        def send(step, carry):
+        piece = size // parts
+
+        def send(turn, carry):
+            step = turn % members
+            first = turn // members * piece
             who = peer(step)
+            mine = ready.at[who, pl.ds(first, piece)]
+            there = buffer.at[pl.ds(pad + me * size + first, piece)]
             near = (step == 0) & (target_section == section)
 
             @pl.when(near)
             def _():
-                pltpu.make_async_copy(
-                    ready.at[who], there, in_recv.at[number]
-                ).start()
+                pltpu.make_async_copy(mine, there, in_recv.at[number]).start()
 
             @pl.when(jnp.logical_not(near))
             def _():
                 pltpu.make_async_remote_copy(
-                    src_ref=ready.at[who],
+                    src_ref=mine,
                     dst_ref=there,
                     send_sem=in_send.at[number],
                     recv_sem=in_recv.at[number],
@@ -178,18 +180,18 @@
 
             return carry
 
-        lax.fori_loop(0, members, send, 0)
-
-    inbound(0, k_ready, k_all, WINDOW, section)
+        lax.fori_loop(0, members * parts, send, 0)
+
+    inbound(0, k_ready, k_all, WINDOW, section, 2)
     loads[1].wait()
     by_group(q_raw, q_ready)
-    inbound(1, q_ready, q_all, 0, section)
+    inbound(1, q_ready, q_all, 0, section, 4)
     loads[2].wait()
     by_group(v_raw, v_ready)
-    inbound(2, v_ready, v_all, WINDOW, section)
+    inbound(2, v_ready, v_all, WINDOW, section, 2)
     loads[3].wait()
     by_group(g_raw, g_ready)
-    inbound(3, g_ready, g_all, 0, behind)
+    inbound(3, g_ready, g_all, 0, behind, 4)
 
     def await_bytes(view, semaphore):
         pltpu.make_async_copy(view, view, semaphore).wait()
@@ -199,6 +201,12 @@
     dk_sum[...] = jnp.zeros(dk_sum.shape, F32)
     dv_sum[...] = jnp.zeros(dv_sum.shape, F32)
 
+    early = tiles // 2 + 1
+    for block in range(early):
+        weights[block, 0 : (tiles - early) * BLOCK, :] = jnp.zeros(
+            ((tiles - early) * BLOCK, lanes), F32
+        )
+
     await_bytes(k_all.at[pl.ds(WINDOW, length)], in_recv.at[0])
 
     def turn(tile, carry):
@@ -210,16 +218,19 @@
 
     await_bytes(q_all, in_recv.at[1])
 
-    def weigh(block, carry):
+    def weigh(first_tile, block, carry):
         first = pl.multiple_of(block * BLOCK, BLOCK)
         query = q_all[pl.ds(pl.multiple_of(block * lanes, lanes), lanes), :]
-        scores = contract(k_all[pl.ds(first, span), :], query, ((1,), (1,)))
+        start = first_tile * BLOCK
+        scores = contract(
+            k_all[pl.ds(first + start, span - start), :], query, ((1,), (1,))
+        )
         key_place = lax.broadcasted_iota(jnp.int32, (BLOCK, lanes), 0)
         lane = lax.broadcasted_iota(jnp.int32, (BLOCK, lanes), 1)
         query_place = lane // (CHUNK * per_group) * CHUNK + lane % CHUNK
         tops = []
-        for tile in range(tiles):
-            part = scores[tile * BLOCK : (tile + 1) * BLOCK, :]
+        for tile in range(first_tile, tiles):
+            part = scores[tile * BLOCK - start : (tile + 1) * BLOCK - start, :]
             if tile == 0:
                 part = jnp.where(key_place > query_place, part, -BIG)
             if tile == tiles - 1:
@@ -229,7 +240,7 @@
             tops.append(jnp.where(tile + block >= tiles - 1, top, -BIG))
         row_max = functools.reduce(jnp.maximum, tops)
         total = jnp.zeros((1, lanes), F32)
-        for tile in range(tiles):
+        for tile in range(first_tile, tiles):
             level = jnp.where(tile + block >= tiles - 1, row_max, BIG)
             part = weights[block, tile * BLOCK : (tile + 1) * BLOCK, :]
             part = jnp.exp2((part - level) * exponent_scale)
@@ -238,7 +249,8 @@
         norms[block] = 1.0 / total
         return carry
 
-    lax.fori_loop(0, blocks, weigh, 0)
+    lax.fori_loop(0, early, functools.partial(weigh, tiles - early), 0)
+    lax.fori_loop(early, blocks, functools.partial(weigh, 0), 0)
 
     await_bytes(v_all.at[pl.ds(WINDOW, length)], in_recv.at[2])
     await_bytes(g_all, in_recv.at[3])
@@ -404,6 +416,18 @@
     await_bytes(others(dv_all), out_send.at[1])
 
 
+def settle(*refs):
+    sources, targets, semaphores = refs[:3], refs[3:6], refs[6]
+    copies = [
+        pltpu.make_async_copy(source, target, semaphores.at[number])
+        for number, (source, target) in enumerate(zip(sources, targets))
+    ]
+    for copy in copies:
+        copy.start()
+    for copy in copies:
+        copy.wait()
+
+
 def solution(mesh):
     sections, members = mesh.shape["section"], mesh.shape["ctx"]
 
@@ -420,13 +444,14 @@
         q_row, kv_row = (rows, heads, width), (rows, groups, width)
         q_sent = (groups, rows * per_group, width)
         kv_sent = (groups, rows, width)
+        results = tuple(
+            jax.ShapeDtypeStruct(shape, BF16) for shape in (q_row, kv_row, kv_row)
+        )
         half = functools.partial(pltpu.VMEM, dtype=BF16)
         full = functools.partial(pltpu.VMEM, dtype=F32)
         dq, dk, dv = pl.pallas_call(
             functools.partial(kernel, sections, members),
-            out_shape=tuple(
-                jax.ShapeDtypeStruct(shape, BF16) for shape in (q_row, kv_row, kv_row)
-            ),
+            out_shape=results,
             in_specs=[outside] * 4,
             out_specs=(inside,) * 3,
             scratch_shapes=[
@@ -478,6 +503,15 @@
                 )
             ),
         )
+        dq, dk, dv = pl.pallas_call(
+            settle,
+            out_shape=results,
+            in_specs=[inside] * 3,
+            out_specs=(outside,) * 3,
+            scratch_shapes=[pltpu.SemaphoreType.DMA((3,))],
+            compiler_params=pltpu.CompilerParams(vmem_limit_bytes=1 << 20),
+            name="settle",
+        )(dq, dk, dv)
         return dq[None], dk[None], dv[None]
 
     spec = P("section", "ctx", None, None)

time: 97.2 us -> 91.6 us (0.942)
  Pallas kernels: 92.6 us -> 89.4 us
  local copies, waits for them, and re-layouts: 2.73 us -> 0 us
    pallas_call x1 -> x2, Pallas kernels: 92.6 us -> 89.4 us  [the longest x1 87.9 us: body(): pl.pallas_call(functools.partial(kernel, sections, members), out_shape=re...]
    unnamed x3 -> x0, local copies, waits for them, and re-layouts: 2.73 us -> none
where the time goes in v3:
time: 91.6 us; the launch traced here: 90 us
  Pallas kernels  89.4 us (98%)
    pallas_call x1, Pallas kernels, body(): pl.pallas_call(functools.partial(kernel, sections, members), out_shape=re...  87.9 us

profile of v3, /device:TPU:96, one launch (start us, length us, event | category | flops | bytes accessed | tf_op | source)
XLA Modules:
  0.0 90.0 jit_solution(4178081996936501430)
XLA Ops:
  0.6 87.9 %relay_attention_backward.1 = (bf16[160,32,128]{2,1,0:T(8,128)(2,1)S(1)}, bf16[160,16,128]{2,1,0:T(8,128)(2,1)S(1)}, bf16[160,16,128]{2,1,0:T(8,128)(2,1)S(1)}) custom-call(bf16[160,32,128]{2,1,0:T(8,128)(2,1)} %bitcast.7, bf16[160,16,128]{2,1,0:T(8,128)(2,1)} %bitcast.9, bf16[160,16,128]{2,1,0:T(8,128)(2,1)} %bitcast.10, bf16[160,32,128]{2,1,0:T(8,128)(2,1)} %bitcast.8), custom_call_target="tpu_custom_call" | custom-call | tf_op jit(solution)/shard_map/relay_attention_backward/pallas_call | solution.py:452
  88.5 1.5 %settle.1 = (bf16[160,32,128]{2,1,0:T(8,128)(2,1)}, bf16[160,16,128]{2,1,0:T(8,128)(2,1)}, bf16[160,16,128]{2,1,0:T(8,128)(2,1)}) custom-call(bf16[160,32,128]{2,1,0:T(8,128)(2,1)S(1)} %get-tuple-element.9.refs_0_, bf16[160,16,128]{2,1,0:T(8,128)(2,1)S(1)} %get-tuple-element.10.refs_1_, bf16[160,16,128]{2,1,0:T(8,128)(2,1)S(1)} %get-tuple-element.11.refs_2_), custom_call_target="tpu_custom_call" | custom-call | tf_op jit(solution)/shard_map/settle/pallas_call | solution.py:506

commit v4 on v3

--- a/solution.py
+++ b/solution.py
@@ -83,8 +83,8 @@
     ahead = (section + 1) % sections
 
     def peer(step):
-        x = (my_x + step) % side
-        y = (my_y + step // side + step) % side
+        x = (my_x + step // side + step) % side
+        y = (my_y + step) % side
         return x * side + y
 
     loads = [
@@ -249,8 +249,8 @@
         norms[block] = 1.0 / total
         return carry
 
-    lax.fori_loop(0, early, functools.partial(weigh, tiles - early), 0)
-    lax.fori_loop(early, blocks, functools.partial(weigh, 0), 0)
+    lax.fori_loop(0, early, functools.partial(weigh, tiles - early), 0, unroll=True)
+    lax.fori_loop(early, blocks, functools.partial(weigh, 0), 0, unroll=3)
 
     await_bytes(v_all.at[pl.ds(WINDOW, length)], in_recv.at[2])
     await_bytes(g_all, in_recv.at[3])
@@ -328,23 +328,29 @@
         dq_all[band, :] = (turned * query_scale).T.astype(BF16)
         return next_dot
 
-    def two_blocks(pair, row_dot):
-        step = 2 * pair
+    def four_blocks(turn, row_dot):
+        step = 4 * turn
         last = blocks - 1
-        row_dot = grads(step, step + 1, grad_probs, next_probs, row_dot)
-        row_dot = grads(
-            step + 1, jnp.minimum(step + 2, last), next_probs, grad_probs, row_dot
-        )
-
-        @pl.when(pair > 0)
+        probs = (grad_probs, next_probs)
+        for offset in range(4):
+            row_dot = grads(
+                step + offset,
+                jnp.minimum(step + offset + 1, last),
+                probs[offset % 2],
+                probs[1 - offset % 2],
+                row_dot,
+            )
+
+        @pl.when(turn > 0)
         def _():
             release(step - 1)
 
-        release(step)
+        for offset in range(3):
+            release(step + offset)
         return row_dot
 
     first_dot = list(look_ahead(0, grad_probs))[-1]
-    lax.fori_loop(0, blocks // 2, two_blocks, first_dot)
+    lax.fori_loop(0, blocks // 4, four_blocks, first_dot)
     release(blocks - 1)
 
     def finish(total, result, scale):
@@ -393,7 +399,7 @@
         )
         return carry
 
-    lax.fori_loop(0, blocks, value_grads, 0)
+    lax.fori_loop(0, blocks, value_grads, 0, unroll=2)
     finish(dv_sum, dv_all, 1.0)
     outbound(1, dv_all, dv_back)
 

time: 91.6 us -> 88.1 us (0.962); the launches traced: 90 us -> 88.1 us
  Pallas kernels: 89.4 us -> 87.4 us
    pallas_call x1, Pallas kernels: 87.9 us -> 85.9 us  [body(): pl.pallas_call(functools.partial(kernel, sections, members), out_shape=re...]
where the time goes in v4:
time: 88.1 us
  Pallas kernels  87.4 us (99%)
    pallas_call x1, Pallas kernels, body(): pl.pallas_call(functools.partial(kernel, sections, members), out_shape=re...  85.9 us

profile of v4, /device:TPU:96, one launch (start us, length us, event | category | flops | bytes accessed | tf_op | source)
XLA Modules:
  0.0 88.1 jit_solution(6859640935768181264)
XLA Ops:
  0.6 85.9 %relay_attention_backward.1 = (bf16[160,32,128]{2,1,0:T(8,128)(2,1)S(1)}, bf16[160,16,128]{2,1,0:T(8,128)(2,1)S(1)}, bf16[160,16,128]{2,1,0:T(8,128)(2,1)S(1)}) custom-call(bf16[160,32,128]{2,1,0:T(8,128)(2,1)} %bitcast.7, bf16[160,16,128]{2,1,0:T(8,128)(2,1)} %bitcast.9, bf16[160,16,128]{2,1,0:T(8,128)(2,1)} %bitcast.10, bf16[160,32,128]{2,1,0:T(8,128)(2,1)} %bitcast.8), custom_call_target="tpu_custom_call" | custom-call | tf_op jit(solution)/shard_map/relay_attention_backward/pallas_call | solution.py:458
  86.5 1.5 %settle.1 = (bf16[160,32,128]{2,1,0:T(8,128)(2,1)}, bf16[160,16,128]{2,1,0:T(8,128)(2,1)}, bf16[160,16,128]{2,1,0:T(8,128)(2,1)}) custom-call(bf16[160,32,128]{2,1,0:T(8,128)(2,1)S(1)} %get-tuple-element.9.refs_0_, bf16[160,16,128]{2,1,0:T(8,128)(2,1)S(1)} %get-tuple-element.10.refs_1_, bf16[160,16,128]{2,1,0:T(8,128)(2,1)S(1)} %get-tuple-element.11.refs_2_), custom_call_target="tpu_custom_call" | custom-call | tf_op jit(solution)/shard_map/settle/pallas_call | solution.py:512
